TPU v7x, 32 devices: a whole 2x2x4 slice. The times are simulated.
32 devices in a mesh: party: 2 (over x), sample: 8 (over z, core), feat: 2 (over y).
Axes of the slice: x: 2, y: 2, z: 4, core: 2. Of those that a mesh axis runs over, the one named last changes fastest.
Arguments:
- x_share: bfloat16 [2, 2048, 8192], P('party', 'sample', 'feat'), may hold values from -3 to 3
- a_share: bfloat16 [2, 2048, 8192], P('party', 'sample', 'feat'), may hold values from -3 to 3
- w_share: float32 [2, 8192, 256], P('party', 'feat'), may hold values from -0.0625 to 0.0625
- b_share: bfloat16 [2, 8192, 256], P('party', 'feat'), may hold values from -0.0625 to 0.0625
- c_share: bfloat16 [2, 2048, 256], P('party', 'sample'), may hold values from -6 to 6
- mask_lin: bfloat16 [2, 2048, 256], P('party', 'sample'), may hold values from -12 to 12
- mask_sq: bfloat16 [2, 2048, 256], P('party', 'sample'), may hold values from -30 to 30
- mask_cube: bfloat16 [2, 2048, 256], P('party', 'sample'), may hold values from -240 to 240
- y_share: bfloat16 [2, 2048, 256], P('party', 'sample'), may hold values from -6 to 6
- r_mask: bfloat16 [2, 2048, 256], P('party', 'sample'), may hold values from -3 to 3
- grad_product: bfloat16 [2, 8192, 256], P('party', 'feat'), may hold values from -240 to 240
Outputs:
- new_weights: float32 [2, 8192, 256], P('party', 'feat')
All inputs are finite; a program needn't handle non-finite values.
Results may differ from a plain program's by a relative error of at most 0.0018.
Values may be sent and summed in bfloat16 or wider, within the bound.
No kernel may reach another device: no remote copies, remote signals or barrier semaphores. Data moves between devices by JAX's collectives and lax.ppermute only.
A program may use at most 64 MiB of HBM per device.

v0:
```python
import jax
import jax.numpy as jnp
from jax import lax
from jax.experimental import pallas as pl
from jax.experimental.pallas import tpu as pltpu
from jax.sharding import PartitionSpec as P


learn_rate = 64.0
slope_one = 0.197
cube_coef = 0.004
input_reach = 3.0
mask_reach = 3.0
chunks = 4

f32 = jnp.float32
bf16 = jnp.bfloat16
f16 = jnp.float16


def swap(value, axes, size, bit):
    return lax.ppermute(value, axes, [(i, i ^ bit) for i in range(size)])


def after(value, token):
    return lax.optimization_barrier((value, token))[0]


def narrow(value, dtype):
    info = jnp.finfo(dtype)
    return lax.reduce_precision(value, info.nexp, info.nmant).astype(dtype)


def opened(p, q):
    return narrow(p.astype(f32) + q.astype(f32), bf16)


def dot(left, right):
    return jnp.dot(left, right, preferred_element_type=f32)


def dot_rows(left, right):
    return lax.dot_general(left, right, (((0,), (0,)), ((), ())), preferred_element_type=f32)


def rows(array, first, number):
    return lax.dynamic_slice_in_dim(array, first, number, 0)


def pack_rows(arrays, block_index, block):
    width = arrays[0].shape[1]

    def body(index, *refs):
        for k, ref in enumerate(refs[:-1]):
            refs[-1][k * block : (k + 1) * block, :] = ref[...]

    spec = pl.BlockSpec((block, width), lambda i, index: (index[0], 0))
    number = len(arrays) * block
    return pl.pallas_call(
        body,
        out_shape=jax.ShapeDtypeStruct((number, width), arrays[0].dtype),
        grid_spec=pltpu.PrefetchScalarGridSpec(
            num_scalar_prefetch=1,
            grid=(1,),
            in_specs=[spec] * len(arrays),
            out_specs=pl.BlockSpec((number, width), lambda i, index: (0, 0)),
        ),
        cost_estimate=pl.CostEstimate(flops=0, bytes_accessed=4 * number * width, transcendentals=0),
        name="pack_rows",
    )(jnp.reshape(block_index, (1,)), *arrays)


def step_fn(x, a, w, b, c_sh, lin, sq, cube, y, r, gp):
    x, a, w, b, gp = x[0], a[0], w[0], b[0], gp[0]
    small = (c_sh[0], lin[0], sq[0], cube[0], y[0], r[0])
    n_sample, n_feat, n_party = (lax.axis_size(k) for k in ("sample", "feat", "party"))
    party, s, feat = (lax.axis_index(k) for k in ("party", "sample", "feat"))
    core = s % 2
    chip = s // 2
    n_chip = n_sample // 2
    group = ("party", "feat")
    n_group = n_party * n_feat
    me = party * n_feat + feat
    samples = x.shape[0]
    pheno = w.shape[1]
    half = x.shape[1] // 2
    quarter = half // 2
    first = core == 0
    select = (party == 0).astype(f32)
    total_samples = samples * n_sample
    rate = learn_rate / total_samples

    def core_swap(v):
        return swap(v, "sample", n_sample, 1)

    def party_swap(v):
        return swap(v, "party", n_party, 1)

    def pick(v):
        return jnp.where(first, v[:, :half], v[:, half:]), jnp.where(first, v[:, half:], v[:, :half])

    slab = half // n_chip
    at = core * half + chip * slab
    w_m = narrow(rows(w, at, slab) - rows(b, at, slab).astype(f32), bf16)
    w_o = party_swap(w_m)

    m = narrow(x.astype(f32) - a.astype(f32), bf16)
    m_mine, m_send = pick(m)
    a_mine, a_send = pick(a)
    m_oth = core_swap(m_send)
    own_a, own_b = m_mine[:, :quarter], m_mine[:, quarter:]
    o_own_a = party_swap(own_a)
    o_oth = party_swap(m_oth)
    o_own_b = party_swap(own_b)
    a_oth = core_swap(a_send)
    r_own = small[5]
    r_oth = core_swap(r_own)

    d_slab = opened(w_m, w_o)
    opened_w = jnp.zeros((half, pheno), bf16)
    opened_w = lax.dynamic_update_slice_in_dim(opened_w, d_slab, chip * slab, 0)
    for j in range(1, n_chip):
        got = swap(d_slab, "sample", n_sample, 2 * j)
        opened_w = lax.dynamic_update_slice_in_dim(opened_w, got, (chip ^ j) * slab, 0)
    b_half = rows(b, core * half, half)
    d_sel = opened_w * select.astype(bf16)

    block = samples // n_group
    packed = party_swap(pack_rows(small, me ^ n_feat, block))
    other_small = [packed[k * block : (k + 1) * block].astype(f32) for k in range(6)]
    own_small = [rows(v, me * block, block).astype(f32) for v in small]

    e_own_a = opened(own_a, o_own_a)
    e_oth = opened(m_oth, o_oth)
    p_oth = dot(e_oth, d_sel) + dot(e_oth, b_half) + dot(a_oth, opened_w)
    e_own_b = opened(own_b, after(o_own_b, p_oth))
    p_sum = dot(a_mine, opened_w) + core_swap(p_oth)
    p_sum = p_sum + dot(e_own_a, d_sel[:quarter]) + dot(e_own_a, b_half[:quarter])
    p_sum = p_sum + dot(e_own_b, d_sel[quarter:]) + dot(e_own_b, b_half[quarter:])

    sums = {0: rows(p_sum, me * block, block)}
    for j in range(1, n_group):
        got = swap(rows(p_sum, (me ^ j) * block, block), group, n_group, j)
        q = j // n_feat
        sums[q] = sums[q] + got if q in sums else got

    def shifted(total, arrays):
        margin = total + arrays[0]
        return margin, margin - arrays[1]

    m_a, d_a = shifted(sums[0], own_small)
    m_b, d_b = shifted(sums[1], other_small)
    spread = d_a + d_b

    def masked_residual(margin, arrays, sel):
        _, l, q, k, lab, mask = arrays
        cubed = sel * (spread * spread * spread) + 3.0 * (spread * spread) * l
        cubed = cubed + 3.0 * spread * q + k
        res = 0.5 * sel + slope_one * margin - cube_coef * cubed - lab
        return narrow(res - mask, bf16)

    res = opened(masked_residual(m_a, own_small, select), masked_residual(m_b, other_small, 1.0 - select))

    res_own = jnp.zeros((samples, pheno), bf16)
    res_own = lax.dynamic_update_slice_in_dim(res_own, res, me * block, 0)
    for j in range(1, n_group):
        got = swap(res, group, n_group, j)
        res_own = lax.dynamic_update_slice_in_dim(res_own, got, (me ^ j) * block, 0)
    res_oth = core_swap(res_own)

    early_oth = dot_rows(e_oth, r_oth)
    early_a = dot_rows(e_own_a, r_own)
    early_b = dot_rows(e_own_b, r_own)
    base = lax.optimization_barrier(w - rate * gp.astype(f32))

    top = jnp.max(jnp.maximum(jnp.abs(res_own), jnp.abs(res_oth)), axis=0, keepdims=True).astype(f32)
    bound = 2 * samples * (5.0 * input_reach * top + 4.0 * input_reach * mask_reach)
    scale = jnp.exp2(jnp.ceil(jnp.log2(bound)) - 15.0)

    def chip_pairs(pairs):
        return [(2 * i + k, 2 * j + k) for i, j in pairs for k in (0, 1)]

    middle = n_chip // 2
    step = half // chunks
    zone = [chip_pairs([(d, d + 1), (n_chip - 1 - d, n_chip - 2 - d)]) for d in range(middle - 1)]
    centre = chip_pairs([(middle - 1, middle), (middle, middle - 1)])
    back = [chip_pairs([(d + 1, d), (n_chip - 2 - d, n_chip - 1 - d)]) for d in range(middle - 1)]

    def share_scale(v, pairs):
        return lax.ppermute(jnp.broadcast_to(v, (8, pheno)), "sample", pairs)[:1]

    rs_own = res_own * select.astype(bf16)
    rs_oth = res_oth * select.astype(bf16)
    vals = []
    token = res_oth
    for k in range(chunks):
        cols = slice(k * step, (k + 1) * step)
        e_part, early_part, off = (e_own_a, early_a, 0) if k < chunks // 2 else (e_own_b, early_b, quarter)
        own = slice(k * step - off, (k + 1) * step - off)
        g = early_oth[cols] + early_part[own] + dot_rows(e_part[:, own], after(rs_own, token))
        g = g + dot_rows(e_oth[:, cols], rs_oth)
        g = g + dot_rows(a_mine[:, cols], res_own)
        g = g + dot_rows(a_oth[:, cols], res_oth)
        v = g * (1.0 / scale)
        token = narrow(v, f16)
        vals.append((v, token))

    msgs = [m for _, m in vals]
    vals = [v for v, _ in vals]
    scales = scale
    inward = []
    for d in range(middle - 1):
        got_scale = share_scale(scales, zone[d])
        wider = 2.0 * jnp.maximum(scales, got_scale)
        inward.append((scales / wider, got_scale / wider))
        scales = wider
    mid_scale = share_scale(scales, centre)
    wider = 2.0 * jnp.maximum(scales, mid_scale)
    keep_mid, take_mid = scales / wider, mid_scale / wider
    final_scale = wider
    for d in reversed(range(middle - 1)):
        got_scale = share_scale(final_scale, back[d])
        outer = (chip == d) | (chip == n_chip - 1 - d)
        final_scale = jnp.where(outer, got_scale, final_scale)
    final_rate = rate * final_scale

    n_in = middle - 1
    stages = [("in", d) for d in range(n_in)] + [("mid", 0)] + [("out", d) for d in reversed(range(n_in))]
    result = base
    flight = {}
    for k in range(chunks):
        kind, d = stages[0]
        flight[k] = lax.ppermute(msgs[k], "sample", zone[d] if kind == "in" else centre)
    order = sorted((k + st, st, k) for k in range(chunks) for st in range(len(stages)))
    for _, st, k in order:
        kind, d = stages[st]
        got = after(flight[k], token)
        if kind == "in":
            keep, take = inward[d]
            vals[k] = vals[k] * keep + got.astype(f32) * take
            msgs[k] = narrow(vals[k], f16)
        elif kind == "mid":
            msgs[k] = narrow(msgs[k].astype(f32) * keep_mid + got.astype(f32) * take_mid, f16)
        else:
            outer = (chip == d) | (chip == n_chip - 1 - d)
            msgs[k] = jnp.where(outer, got, msgs[k])
        token = msgs[k]
        if st + 1 < len(stages):
            kind, d = stages[st + 1]
            pairs = zone[d] if kind == "in" else centre if kind == "mid" else back[d]
            flight[k] = lax.ppermute(msgs[k], "sample", pairs)
        else:
            theirs = core_swap(msgs[k])
            for value, who in ((msgs[k], core), (theirs, 1 - core)):
                where = who * half + k * step
                new = rows(result, where, step) - final_rate * value.astype(f32)
                result = lax.dynamic_update_slice_in_dim(result, new, where, 0)
    return result[None]


def solution(mesh):
    placed = (
        P("party", "sample", "feat"),
        P("party", "sample", "feat"),
        P("party", "feat", None),
        P("party", "feat", None),
        P("party", "sample", None),
        P("party", "sample", None),
        P("party", "sample", None),
        P("party", "sample", None),
        P("party", "sample", None),
        P("party", "sample", None),
        P("party", "feat", None),
    )
    return jax.shard_map(step_fn, mesh=mesh, in_specs=placed, out_specs=P("party", "feat", None), check_vma=False)
```

profile of v0, /device:TPU:0, one launch (start us, length us, event | category | flops | bytes accessed | tf_op | source)
XLA Modules:
  0.0 190.6 jit_solution(15079304603413875723)
XLA Ops:
  1.2 3.0 %collective-permute-start = (bf16[512,256]{1,0:T(8,128)(2,1)S(1)}, bf16[512,256]{1,0:T(8,128)(2,1)}, u32[]{:S(2)}, u32[]{:S(2)}) collective-permute-start(bf16[512,256]{1,0:T(8,128)(2,1)S(1)} %fusion.32), channel_id=1, source_target_pairs={{0,16},{16,0},{1,17},{17,1},{2,18},{18,2},{3,19},{19,3},{4,20},{20... | collective-permute-start | bytes 786440 | tf_op jit(solution)/shard_map/ppermute | solution.py:22
  4.2 3.2 %fusion.1 = bf16[256,4096]{1,0:T(8,128)(2,1)S(1)} fusion(bf16[1,256,4096]{2,1,0:T(8,128)(2,1)} %param.11, bf16[1,256,4096]{2,1,0:T(8,128)(2,1)} %param.12), kind=kLoop, calls=%fused_computation.2 | loop fusion | flops 5242880 | bytes 6291456 | tf_op jit(solution)/shard_map/convert_element_type | solution.py:31
  11.0 2.4 %subtract_bitcast_fusion = f32[4096,256]{1,0:T(8,128)} fusion(f32[1,4096,256]{2,1,0:T(8,128)S(1)} %copy-done.1, bf16[1,4096,256]{2,1,0:T(8,128)(2,1)S(1)} %copy-done.3), kind=kLoop, calls=%fused_computation.3 | loop fusion | flops 3145728 | bytes 10485760 | tf_op jit(solution)/shard_map/sub | solution.py:174
  15.2 2.6 %collective-permute-start.2 = (bf16[512,256]{1,0:T(8,128)(2,1)}, bf16[512,256]{1,0:T(8,128)(2,1)}, u32[]{:S(2)}, u32[]{:S(2)}) collective-permute-start(bf16[512,256]{1,0:T(8,128)(2,1)} %get-tuple-element.56), channel_id=1, source_target_pairs={{0,8},{2,10},{4,12},{6,14},{8,0},{10,2},{12,4},{14,6},{1,9},{3,11}... | collective-permute-start | bytes 786440 | tf_op jit(solution)/shard_map/ppermute | solution.py:22
  22.3 8.2 %collective-permute-done.1 = bf16[512,256]{1,0:T(8,128)(2,1)} collective-permute-done((bf16[512,256]{1,0:T(8,128)(2,1)}, bf16[512,256]{1,0:T(8,128)(2,1)}, u32[]{:S(2)}, u32[]{:S(2)}) %collective-permute-start.1) | collective-permute-done | bytes 262176 | tf_op jit(solution)/shard_map/ppermute | solution.py:22
  40.0 16.8 %collective-permute-done.5 = bf16[256,2048]{1,0:T(8,128)(2,1)S(1)} collective-permute-done((bf16[256,2048]{1,0:T(8,128)(2,1)}, bf16[256,2048]{1,0:T(8,128)(2,1)S(1)}, u32[]{:S(2)}, u32[]{:S(2)}) %collective-permute-start.5) | collective-permute-done | bytes 1048608 | tf_op jit(solution)/shard_map/ppermute | solution.py:22
  59.4 23.6 %collective-permute-done.9 = bf16[256,1024]{1,0:T(8,128)(2,1)S(1)} collective-permute-done((bf16[256,1024]{1,0:T(8,128)(2,1)}, bf16[256,1024]{1,0:T(8,128)(2,1)S(1)}, u32[]{:S(2)}, u32[]{:S(2)}) %collective-permute-start.9) | collective-permute-done | bytes 524320 | tf_op jit(solution)/shard_map/ppermute | solution.py:22
  89.9 2.4 %collective-permute-done.12 = f32[64,256]{1,0:T(8,128)S(1)} collective-permute-done((f32[64,256]{1,0:T(8,128)S(1)}, f32[64,256]{1,0:T(8,128)S(1)}, u32[]{:S(2)}, u32[]{:S(2)}) %collective-permute-start.12) | collective-permute-done | bytes 65568 | tf_op jit(solution)/shard_map/ppermute | solution.py:22
  99.0 2.2 %collective-permute-done.16 = bf16[64,256]{1,0:T(8,128)(2,1)S(1)} collective-permute-done((bf16[64,256]{1,0:T(8,128)(2,1)S(1)}, bf16[64,256]{1,0:T(8,128)(2,1)S(1)}, u32[]{:S(2)}, u32[]{:S(2)}) %collective-permute-start.16) | collective-permute-done | bytes 32800 | tf_op jit(solution)/shard_map/ppermute | solution.py:22
  106.8 4.4 %collective-permute-start.24 = (f16[512,256]{1,0:T(8,128)(2,1)S(1)}, f16[512,256]{1,0:T(8,128)(2,1)S(1)}, u32[]{:S(2)}, u32[]{:S(2)}) collective-permute-start(f16[512,256]{1,0:T(8,128)(2,1)S(1)} %get-tuple-element.75), channel_id=1, source_target_pairs={{0,4},{2,6},{12,8},{14,10},{1,5},{3,7},{13,9},{15,11},{16,20},{18,... | collective-permute-start | bytes 786440 | tf_op jit(solution)/shard_map/ppermute | solution.py:233
  118.7 9.9 %collective-permute-done.18 = f32[8,256]{1,0:T(8,128)S(1)} collective-permute-done((f32[8,256]{1,0:T(8,128)S(1)}, f32[8,256]{1,0:T(8,128)S(1)}, u32[]{:S(2)}, u32[]{:S(2)}) %collective-permute-start.18) | collective-permute-done | bytes 8224 | tf_op jit(solution)/shard_map/ppermute | solution.py:190
  129.8 6.3 %collective-permute-start.31 = (f16[512,256]{1,0:T(8,128)(2,1)S(1)}, f16[512,256]{1,0:T(8,128)(2,1)S(1)}, u32[]{:S(2)}, u32[]{:S(2)}) collective-permute-start(f16[512,256]{1,0:T(8,128)(2,1)S(1)} %get-tuple-element.79), channel_id=1, source_target_pairs={{0,4},{2,6},{12,8},{14,10},{1,5},{3,7},{13,9},{15,11},{16,20},{18,... | collective-permute-start | bytes 786440 | tf_op jit(solution)/shard_map/ppermute | solution.py:233
  138.4 3.2 %collective-permute-done.20 = f32[8,256]{1,0:T(8,128)S(1)} collective-permute-done((f32[8,256]{1,0:T(8,128)S(1)}, f32[8,256]{1,0:T(8,128)S(1)}, u32[]{:S(2)}, u32[]{:S(2)}) %collective-permute-start.20) | collective-permute-done | bytes 8224 | tf_op jit(solution)/shard_map/ppermute | solution.py:190
  147.1 11.7 %collective-permute-done.25 = f16[512,256]{1,0:T(8,128)(2,1)S(1)} collective-permute-done((f16[512,256]{1,0:T(8,128)(2,1)S(1)}, f16[512,256]{1,0:T(8,128)(2,1)S(1)}, u32[]{:S(2)}, u32[]{:S(2)}) %collective-permute-start.25) | collective-permute-done | bytes 262176 | tf_op jit(solution)/shard_map/ppermute | solution.py:251
  158.8 2.0 %subtract_dynamic-update-slice_fusion.6 = (f32[4096,256]{1,0:T(8,128)}, f16[512,256]{1,0:T(8,128)(2,1)S(1)}) fusion(f32[4096,256]{1,0:T(8,128)} %subtract_bitcast_fusion, s32[]{:T(128)S(6)} %select_n.131, f32[256]{0:T(256)S(1)} %bitcast.114, f16[512,256]{1,0:T(8,128)(2,1)S(1)} %collective-permute-done.25, ...), kind=kLoop, calls=%fused_computation.61 | loop fusion | flops 524288 | bytes 1836037 | tf_op jit(solution)/shard_map/dynamic_update_slice | solution.py:257
  163.5 1.9 %subtract_dynamic-update-slice_fusion.5 = f32[4096,256]{1,0:T(8,128)} fusion(f32[4096,256]{1,0:T(8,128)} %get-tuple-element.45, s32[]{:T(128)S(6)} %select_n.151, f16[512,256]{1,0:T(8,128)(2,1)S(1)} %collective-permute-done.28, f32[256]{0:T(256)S(1)} %bitcast.115), kind=kLoop, calls=%fused_computation.60 | loop fusion | flops 393216 | bytes 1311748 | tf_op jit(solution)/shard_map/dynamic_update_slice | solution.py:257
  165.4 1.9 %subtract_dynamic-update-slice_fusion.4 = (f32[4096,256]{1,0:T(8,128)}, f16[512,256]{1,0:T(8,128)(2,1)S(1)}) fusion(f32[4096,256]{1,0:T(8,128)} %subtract_dynamic-update-slice_fusion.5, s32[]{:T(128)S(6)} %select_n.152, f32[256]{0:T(256)S(1)} %bitcast.116, f16[512,256]{1,0:T(8,128)(2,1)S(1)} %collective-permute-done.29, ...), kind=kLoop, calls=%fused_computation.57 | loop fusion | flops 524288 | bytes 1836037 | tf_op jit(solution)/shard_map/dynamic_update_slice | solution.py:257
  169.6 4.2 %collective-permute-done.33 = f16[512,256]{1,0:T(8,128)(2,1)S(1)} collective-permute-done((f16[512,256]{1,0:T(8,128)(2,1)S(1)}, f16[512,256]{1,0:T(8,128)(2,1)S(1)}, u32[]{:S(2)}, u32[]{:S(2)}) %collective-permute-start.33) | collective-permute-done | bytes 262176 | tf_op jit(solution)/shard_map/ppermute | solution.py:251
  173.8 1.9 subtract_dynamic-update-slice_fusion.3
  175.7 1.9 %subtract_dynamic-update-slice_fusion.2 = (f32[4096,256]{1,0:T(8,128)}, f16[512,256]{1,0:T(8,128)(2,1)S(1)}) fusion(f32[4096,256]{1,0:T(8,128)} %subtract_dynamic-update-slice_fusion.3, s32[]{:T(128)S(6)} %select_n.155, f32[256]{0:T(256)S(1)} %bitcast.118, f16[512,256]{1,0:T(8,128)(2,1)S(1)} %collective-permute-done.33, ...), kind=kLoop, calls=%fused_computation.54 | loop fusion | flops 524288 | bytes 1836037 | tf_op jit(solution)/shard_map/dynamic_update_slice | solution.py:257
  177.6 2.8 %collective-permute-done.36 = f16[512,256]{1,0:T(8,128)(2,1)S(1)} collective-permute-done((f16[512,256]{1,0:T(8,128)(2,1)S(1)}, f16[512,256]{1,0:T(8,128)(2,1)S(1)}, u32[]{:S(2)}, u32[]{:S(2)}) %collective-permute-start.36) | collective-permute-done | bytes 262176 | tf_op jit(solution)/shard_map/ppermute | solution.py:251
  182.3 2.0 %subtract_dynamic-update-slice_fusion = (f32[4096,256]{1,0:T(8,128)}, f16[512,256]{1,0:T(8,128)(2,1)S(1)}) fusion(f32[4096,256]{1,0:T(8,128)} %subtract_dynamic-update-slice_fusion.1, s32[]{:T(128)S(6)} %select_n.158, f32[256]{0:T(256)S(1)} %bitcast.120, f16[512,256]{1,0:T(8,128)(2,1)S(1)} %collective-permute-done.36, ...), kind=kLoop, calls=%fused_computation.52 | loop fusion | flops 524288 | bytes 1836037 | tf_op jit(solution)/shard_map/dynamic_update_slice | solution.py:257
  184.3 4.5 %copy.27 = f32[1,4096,256]{2,1,0:T(8,128)} copy(f32[1,4096,256]{2,1,0:T(8,128)} %bitcast.29) | data formatting | bytes 8388608
  188.7 1.9 bitcast_dynamic-update-slice_fusion
  (135 shorter events, 65.2 us)
Async XLA Ops:
  1.2 12.2 %collective-permute-start = (bf16[512,256]{1,0:T(8,128)(2,1)S(1)}, bf16[512,256]{1,0:T(8,128)(2,1)}, u32[]{:S(2)}, u32[]{:S(2)}) collective-permute-start(bf16[512,256]{1,0:T(8,128)(2,1)S(1)} %fusion.32), channel_id=1, source_target_pairs={{0,16},{16,0},{1,17},{17,1},{2,18},{18,2},{3,19},{19,3},{4,20},{20... | collective-permute-start | bytes 786440 | tf_op jit(solution)/shard_map/ppermute | solution.py:22
  8.5 22.0 %collective-permute-start.4 = (bf16[256,2048]{1,0:T(8,128)(2,1)}, bf16[256,2048]{1,0:T(8,128)(2,1)}, u32[]{:S(2)}, u32[]{:S(2)}) collective-permute-start(bf16[256,2048]{1,0:T(8,128)(2,1)} %get-tuple-element.59), channel_id=1, source_target_pairs={{0,2},{2,0},{4,6},{6,4},{8,10},{10,8},{12,14},{14,12},{1,3},{3,1},... | collective-permute-start | bytes 3145736 | tf_op jit(solution)/shard_map/ppermute | solution.py:22
  9.6 27.1 %collective-permute-start.6 = (bf16[256,2048]{1,0:T(8,128)(2,1)}, bf16[256,2048]{1,0:T(8,128)(2,1)}, u32[]{:S(2)}, u32[]{:S(2)}) collective-permute-start(bf16[256,2048]{1,0:T(8,128)(2,1)} %get-tuple-element.58), channel_id=1, source_target_pairs={{0,2},{2,0},{4,6},{6,4},{8,10},{10,8},{12,14},{14,12},{1,3},{3,1},... | collective-permute-start | bytes 3145736 | tf_op jit(solution)/shard_map/ppermute | solution.py:22
  15.2 17.1 %collective-permute-start.2 = (bf16[512,256]{1,0:T(8,128)(2,1)}, bf16[512,256]{1,0:T(8,128)(2,1)}, u32[]{:S(2)}, u32[]{:S(2)}) collective-permute-start(bf16[512,256]{1,0:T(8,128)(2,1)} %get-tuple-element.56), channel_id=1, source_target_pairs={{0,8},{2,10},{4,12},{6,14},{8,0},{10,2},{12,4},{14,6},{1,9},{3,11}... | collective-permute-start | bytes 786440 | tf_op jit(solution)/shard_map/ppermute | solution.py:22
  17.8 12.7 %collective-permute-start.1 = (bf16[512,256]{1,0:T(8,128)(2,1)}, bf16[512,256]{1,0:T(8,128)(2,1)}, u32[]{:S(2)}, u32[]{:S(2)}) collective-permute-start(bf16[512,256]{1,0:T(8,128)(2,1)} %get-tuple-element.56), channel_id=1, source_target_pairs={{0,4},{2,6},{4,0},{6,2},{8,12},{10,14},{12,8},{14,10},{1,5},{3,7},... | collective-permute-start | bytes 786440 | tf_op jit(solution)/shard_map/ppermute | solution.py:22
  19.4 16.7 %collective-permute-start.3 = (bf16[512,256]{1,0:T(8,128)(2,1)}, bf16[512,256]{1,0:T(8,128)(2,1)S(1)}, u32[]{:S(2)}, u32[]{:S(2)}) collective-permute-start(bf16[512,256]{1,0:T(8,128)(2,1)} %get-tuple-element.56), channel_id=1, source_target_pairs={{0,12},{2,14},{4,8},{6,10},{8,4},{10,6},{12,0},{14,2},{1,13},{3,15... | collective-permute-start | bytes 786440 | tf_op jit(solution)/shard_map/ppermute | solution.py:22
  30.5 53.5 %collective-permute-start.21 = (bf16[256,256]{1,0:T(8,128)(2,1)S(1)}, bf16[256,256]{1,0:T(8,128)(2,1)S(1)}, u32[]{:S(2)}, u32[]{:S(2)}) collective-permute-start(bf16[256,256]{1,0:T(8,128)(2,1)S(1)} %bitcast.108), channel_id=1, source_target_pairs={{0,2},{2,0},{4,6},{6,4},{8,10},{10,8},{12,14},{14,12},{1,3},{3,1},... | collective-permute-start | bytes 393224 | tf_op jit(solution)/shard_map/ppermute | solution.py:22
  30.5 26.3 %collective-permute-start.5 = (bf16[256,2048]{1,0:T(8,128)(2,1)}, bf16[256,2048]{1,0:T(8,128)(2,1)S(1)}, u32[]{:S(2)}, u32[]{:S(2)}) collective-permute-start(bf16[256,2048]{1,0:T(8,128)(2,1)} %collective-permute-done.4), channel_id=1, source_target_pairs={{0,16},{16,0},{1,17},{17,1},{2,18},{18,2},{3,19},{19,3},{4,20},{20... | collective-permute-start | bytes 3145736 | tf_op jit(solution)/shard_map/ppermute | solution.py:22
  32.3 57.2 %collective-permute-start.13 = (bf16[384,256]{1,0:T(8,128)(2,1)}, bf16[384,256]{1,0:T(8,128)(2,1)S(1)}, u32[]{:S(2)}, u32[]{:S(2)}) collective-permute-start(bf16[384,256]{1,0:T(8,128)(2,1)} %pack_rows.1), channel_id=1, source_target_pairs={{0,16},{16,0},{1,17},{17,1},{2,18},{18,2},{3,19},{19,3},{4,20},{20... | collective-permute-start | bytes 589832 | tf_op jit(solution)/shard_map/ppermute | solution.py:22
  36.1 46.8 %collective-permute-start.8 = (bf16[256,1024]{1,0:T(8,128)(2,1)}, bf16[256,1024]{1,0:T(8,128)(2,1)S(1)}, u32[]{:S(2)}, u32[]{:S(2)}) collective-permute-start(bf16[256,1024]{1,0:T(8,128)(2,1)} %get-tuple-element.63), channel_id=1, source_target_pairs={{0,16},{16,0},{1,17},{17,1},{2,18},{18,2},{3,19},{19,3},{4,20},{20... | collective-permute-start | bytes 1572872 | tf_op jit(solution)/shard_map/ppermute | solution.py:22
  36.8 46.2 %collective-permute-start.9 = (bf16[256,1024]{1,0:T(8,128)(2,1)}, bf16[256,1024]{1,0:T(8,128)(2,1)S(1)}, u32[]{:S(2)}, u32[]{:S(2)}) collective-permute-start(bf16[256,1024]{1,0:T(8,128)(2,1)} %get-tuple-element.64), channel_id=1, source_target_pairs={{0,16},{16,0},{1,17},{17,1},{2,18},{18,2},{3,19},{19,3},{4,20},{20... | collective-permute-start | bytes 1572872 | tf_op jit(solution)/shard_map/ppermute | solution.py:22
  59.3 25.8 %collective-permute-start.7 = (f32[256,256]{1,0:T(8,128)S(1)}, f32[256,256]{1,0:T(8,128)S(1)}, u32[]{:S(2)}, u32[]{:S(2)}) collective-permute-start(f32[256,256]{1,0:T(8,128)S(1)} %add_add_fusion), channel_id=1, source_target_pairs={{0,2},{2,0},{4,6},{6,4},{8,10},{10,8},{12,14},{14,12},{1,3},{3,1},... | collective-permute-start | bytes 786440 | tf_op jit(solution)/shard_map/ppermute | solution.py:22
  106.8 34.9 %collective-permute-start.24 = (f16[512,256]{1,0:T(8,128)(2,1)S(1)}, f16[512,256]{1,0:T(8,128)(2,1)S(1)}, u32[]{:S(2)}, u32[]{:S(2)}) collective-permute-start(f16[512,256]{1,0:T(8,128)(2,1)S(1)} %get-tuple-element.75), channel_id=1, source_target_pairs={{0,4},{2,6},{12,8},{14,10},{1,5},{3,7},{13,9},{15,11},{16,20},{18,... | collective-permute-start | bytes 786440 | tf_op jit(solution)/shard_map/ppermute | solution.py:233
  111.2 26.2 %collective-permute-start.22 = (f16[512,256]{1,0:T(8,128)(2,1)S(1)}, f16[512,256]{1,0:T(8,128)(2,1)S(1)}, u32[]{:S(2)}, u32[]{:S(2)}) collective-permute-start(f16[512,256]{1,0:T(8,128)(2,1)S(1)} %get-tuple-element.73), channel_id=1, source_target_pairs={{0,4},{2,6},{12,8},{14,10},{1,5},{3,7},{13,9},{15,11},{16,20},{18,... | collective-permute-start | bytes 786440 | tf_op jit(solution)/shard_map/ppermute | solution.py:233
  114.6 29.8 %collective-permute-start.27 = (f16[512,256]{1,0:T(8,128)(2,1)S(1)}, f16[512,256]{1,0:T(8,128)(2,1)S(1)}, u32[]{:S(2)}, u32[]{:S(2)}) collective-permute-start(f16[512,256]{1,0:T(8,128)(2,1)S(1)} %get-tuple-element.77), channel_id=1, source_target_pairs={{0,4},{2,6},{12,8},{14,10},{1,5},{3,7},{13,9},{15,11},{16,20},{18,... | collective-permute-start | bytes 786440 | tf_op jit(solution)/shard_map/ppermute | solution.py:233
  115.9 12.7 %collective-permute-start.18 = (f32[8,256]{1,0:T(8,128)S(1)}, f32[8,256]{1,0:T(8,128)S(1)}, u32[]{:S(2)}, u32[]{:S(2)}) collective-permute-start(f32[8,256]{1,0:T(8,128)S(1)} %broadcast_in_dim.33), channel_id=1, source_target_pairs={{0,4},{2,6},{12,8},{14,10},{1,5},{3,7},{13,9},{15,11},{16,20},{18,... | collective-permute-start | bytes 24584 | tf_op jit(solution)/shard_map/ppermute | solution.py:190
  128.6 7.5 %collective-permute-start.19 = (f32[8,256]{1,0:T(8,128)S(1)}, f32[8,256]{1,0:T(8,128)S(1)}, u32[]{:S(2)}, u32[]{:S(2)}) collective-permute-start(f32[8,256]{1,0:T(8,128)S(1)} %broadcast_in_dim.35), channel_id=1, source_target_pairs={{4,8},{6,10},{8,4},{10,6},{5,9},{7,11},{9,5},{11,7},{20,24},{22,26... | collective-permute-start | bytes 24584 | tf_op jit(solution)/shard_map/ppermute | solution.py:190
  129.8 31.0 %collective-permute-start.31 = (f16[512,256]{1,0:T(8,128)(2,1)S(1)}, f16[512,256]{1,0:T(8,128)(2,1)S(1)}, u32[]{:S(2)}, u32[]{:S(2)}) collective-permute-start(f16[512,256]{1,0:T(8,128)(2,1)S(1)} %get-tuple-element.79), channel_id=1, source_target_pairs={{0,4},{2,6},{12,8},{14,10},{1,5},{3,7},{13,9},{15,11},{16,20},{18,... | collective-permute-start | bytes 786440 | tf_op jit(solution)/shard_map/ppermute | solution.py:233
  143.1 15.7 %collective-permute-start.25 = (f16[512,256]{1,0:T(8,128)(2,1)S(1)}, f16[512,256]{1,0:T(8,128)(2,1)S(1)}, u32[]{:S(2)}, u32[]{:S(2)}) collective-permute-start(f16[512,256]{1,0:T(8,128)(2,1)S(1)} %reduce-precision_convert_fusion.8), channel_id=1, source_target_pairs={{4,0},{6,2},{8,12},{10,14},{5,1},{7,3},{9,13},{11,15},{20,16},{22,... | collective-permute-start | bytes 786440 | tf_op jit(solution)/shard_map/ppermute | solution.py:251
  144.7 17.1 %collective-permute-start.30 = (f16[512,256]{1,0:T(8,128)(2,1)S(1)}, f16[512,256]{1,0:T(8,128)(2,1)S(1)}, u32[]{:S(2)}, u32[]{:S(2)}) collective-permute-start(f16[512,256]{1,0:T(8,128)(2,1)S(1)} %reduce-precision_convert_fusion.7), channel_id=1, source_target_pairs={{4,8},{6,10},{8,4},{10,6},{5,9},{7,11},{9,5},{11,7},{20,24},{22,26... | collective-permute-start | bytes 786440 | tf_op jit(solution)/shard_map/ppermute | solution.py:251
  145.8 17.7 %collective-permute-start.29 = (f16[512,256]{1,0:T(8,128)(2,1)S(1)}, f16[512,256]{1,0:T(8,128)(2,1)S(1)}, u32[]{:S(2)}, u32[]{:S(2)}) collective-permute-start(f16[512,256]{1,0:T(8,128)(2,1)S(1)} %reduce-precision_convert_fusion.6), channel_id=1, source_target_pairs={{4,0},{6,2},{8,12},{10,14},{5,1},{7,3},{9,13},{11,15},{20,16},{22,... | collective-permute-start | bytes 786440 | tf_op jit(solution)/shard_map/ppermute | solution.py:251
  161.1 6.8 %collective-permute-start.34 = (f16[512,256]{1,0:T(8,128)(2,1)S(1)}, f16[512,256]{1,0:T(8,128)(2,1)S(1)}, u32[]{:S(2)}, u32[]{:S(2)}) collective-permute-start(f16[512,256]{1,0:T(8,128)(2,1)S(1)} %reduce-precision_convert_fusion.5), channel_id=1, source_target_pairs={{4,8},{6,10},{8,4},{10,6},{5,9},{7,11},{9,5},{11,7},{20,24},{22,26... | collective-permute-start | bytes 786440 | tf_op jit(solution)/shard_map/ppermute | solution.py:251
  162.2 11.6 %collective-permute-start.33 = (f16[512,256]{1,0:T(8,128)(2,1)S(1)}, f16[512,256]{1,0:T(8,128)(2,1)S(1)}, u32[]{:S(2)}, u32[]{:S(2)}) collective-permute-start(f16[512,256]{1,0:T(8,128)(2,1)S(1)} %reduce-precision_convert_fusion.4), channel_id=1, source_target_pairs={{4,0},{6,2},{8,12},{10,14},{5,1},{7,3},{9,13},{11,15},{20,16},{22,... | collective-permute-start | bytes 786440 | tf_op jit(solution)/shard_map/ppermute | solution.py:251
  168.3 12.1 %collective-permute-start.36 = (f16[512,256]{1,0:T(8,128)(2,1)S(1)}, f16[512,256]{1,0:T(8,128)(2,1)S(1)}, u32[]{:S(2)}, u32[]{:S(2)}) collective-permute-start(f16[512,256]{1,0:T(8,128)(2,1)S(1)} %reduce-precision_convert_fusion.3), channel_id=1, source_target_pairs={{4,0},{6,2},{8,12},{10,14},{5,1},{7,3},{9,13},{11,15},{20,16},{22,... | collective-permute-start | bytes 786440 | tf_op jit(solution)/shard_map/ppermute | solution.py:251
  (19 other events, 110.3 us)
where the time goes:
time: 192 us; the launch traced here: 191 us
  waiting for transfers between devices  89.1 us (46%)
  starting transfers between devices  44.1 us (23%)
  other arithmetic  32.1 us (17%)
  matrix products  14.7 us (8%)
  local copies, waits for them, and re-layouts  8.57 us (4%)
    ppermute x23, waiting for transfers between devices, swap(): return lax.ppermute(value, axes, [(i, i ^ bit) for i in range(size)])  57.4 us
    ppermute x23, starting transfers between devices, swap(): return lax.ppermute(value, axes, [(i, i ^ bit) for i in range(size)])  19.7 us
    ppermute x8, waiting for transfers between devices, step_fn(): flight[k] = lax.ppermute(msgs[k], 'sample', pairs)  18.7 us
    dynamic_update_slice x8, other arithmetic, step_fn(): result = lax.dynamic_update_slice_in_dim(result, new, where, 0)  15.5 us
    ppermute x4, starting transfers between devices, step_fn(): lax.ppermute(msgs[k], 'sample', zone[d] if kind == 'in' else centre)  13.3 us
    ppermute x3, waiting for transfers between devices, share_scale(): return lax.ppermute(jnp.broadcast_to(v, (8, pheno)), 'sample', pairs)[:1]  13.1 us
    dot_general x19, matrix products, dot_rows(): lax.dot_general(left, right, (((0,), (0,)), ((), ())), preferred_element_...  10.4 us
    convert_element_type x12, other arithmetic, narrow(): return lax.reduce_precision(value, info.nexp, info.nmant).astype(dtype)  9.11 us
  transfers between devices with their start and end apart: 38, of which 15 were waited for; matrix products, arithmetic and copies ran while one was open for 22% of the time, Pallas kernels for 1%

commit v1 on v0

--- a/solution.py
+++ b/solution.py
@@ -126,16 +126,21 @@
     d_sel = opened_w * select.astype(bf16)
 
     block = samples // n_group
-    packed = party_swap(pack_rows(small, me ^ n_feat, block))
+    base = w - rate * gp.astype(f32)
+    packed = pack_rows(small, me ^ n_feat, block)
+    packed, base = lax.optimization_barrier((packed, base))
+    packed = party_swap(packed)
     other_small = [packed[k * block : (k + 1) * block].astype(f32) for k in range(6)]
     own_small = [rows(v, me * block, block).astype(f32) for v in small]
 
     e_own_a = opened(own_a, o_own_a)
     e_oth = opened(m_oth, o_oth)
     p_oth = dot(e_oth, d_sel) + dot(e_oth, b_half) + dot(a_oth, opened_w)
-    e_own_b = opened(own_b, after(o_own_b, p_oth))
-    p_sum = dot(a_mine, opened_w) + core_swap(p_oth)
-    p_sum = p_sum + dot(e_own_a, d_sel[:quarter]) + dot(e_own_a, b_half[:quarter])
+    p_own = dot(a_mine, opened_w) + dot(e_own_a, d_sel[:quarter]) + dot(e_own_a, b_half[:quarter])
+    early_oth = dot_rows(e_oth, r_oth)
+    early_a = dot_rows(e_own_a, r_own)
+    e_own_b = opened(own_b, after(o_own_b, (p_oth, p_own, early_oth, early_a)))
+    p_sum = p_own + core_swap(p_oth)
     p_sum = p_sum + dot(e_own_b, d_sel[quarter:]) + dot(e_own_b, b_half[quarter:])
 
     sums = {0: rows(p_sum, me * block, block)}
@@ -168,10 +173,7 @@
         res_own = lax.dynamic_update_slice_in_dim(res_own, got, (me ^ j) * block, 0)
     res_oth = core_swap(res_own)
 
-    early_oth = dot_rows(e_oth, r_oth)
-    early_a = dot_rows(e_own_a, r_own)
     early_b = dot_rows(e_own_b, r_own)
-    base = lax.optimization_barrier(w - rate * gp.astype(f32))
 
     top = jnp.max(jnp.maximum(jnp.abs(res_own), jnp.abs(res_oth)), axis=0, keepdims=True).astype(f32)
     bound = 2 * samples * (5.0 * input_reach * top + 4.0 * input_reach * mask_reach)
@@ -192,15 +194,16 @@
     rs_own = res_own * select.astype(bf16)
     rs_oth = res_oth * select.astype(bf16)
     vals = []
-    token = res_oth
+    token = res
     for k in range(chunks):
         cols = slice(k * step, (k + 1) * step)
         e_part, early_part, off = (e_own_a, early_a, 0) if k < chunks // 2 else (e_own_b, early_b, quarter)
         own = slice(k * step - off, (k + 1) * step - off)
-        g = early_oth[cols] + early_part[own] + dot_rows(e_part[:, own], after(rs_own, token))
-        g = g + dot_rows(e_oth[:, cols], rs_oth)
-        g = g + dot_rows(a_mine[:, cols], res_own)
-        g = g + dot_rows(a_oth[:, cols], res_oth)
+        s_own, s_oth, f_own, f_oth = after((rs_own, rs_oth, res_own, res_oth), token)
+        g = early_oth[cols] + early_part[own] + dot_rows(e_part[:, own], s_own)
+        g = g + dot_rows(a_mine[:, cols], f_own)
+        g = g + dot_rows(e_oth[:, cols], s_oth)
+        g = g + dot_rows(a_oth[:, cols], f_oth)
         v = g * (1.0 / scale)
         token = narrow(v, f16)
         vals.append((v, token))
@@ -226,7 +229,7 @@
 
     n_in = middle - 1
     stages = [("in", d) for d in range(n_in)] + [("mid", 0)] + [("out", d) for d in reversed(range(n_in))]
-    result = base
+    theirs = []
     flight = {}
     for k in range(chunks):
         kind, d = stages[0]
@@ -250,11 +253,12 @@
             pairs = zone[d] if kind == "in" else centre if kind == "mid" else back[d]
             flight[k] = lax.ppermute(msgs[k], "sample", pairs)
         else:
-            theirs = core_swap(msgs[k])
-            for value, who in ((msgs[k], core), (theirs, 1 - core)):
-                where = who * half + k * step
-                new = rows(result, where, step) - final_rate * value.astype(f32)
-                result = lax.dynamic_update_slice_in_dim(result, new, where, 0)
+            theirs.append(core_swap(msgs[k]))
+    mine = jnp.concatenate([msgs[k] for k in range(chunks)], 0)
+    theirs = jnp.concatenate(theirs, 0)
+    low = jnp.where(first, mine, theirs).astype(f32)
+    high = jnp.where(first, theirs, mine).astype(f32)
+    result = base - final_rate * jnp.concatenate([low, high], 0)
     return result[None]
 
 

time: 192 us -> 167 us (0.87)
  other arithmetic: 32.1 us -> 20.7 us
  waiting for transfers between devices: 89.1 us -> 81 us
  starting transfers between devices: 44.1 us -> 42 us
    dynamic_update_slice x8 -> x0, other arithmetic: 15.5 us -> none  [step_fn(): result = lax.dynamic_update_slice_in_dim(result, new, where, 0)]
    ppermute x3, waiting for transfers between devices: 13.1 us -> 3.21 us  [share_scale(): return lax.ppermute(jnp.broadcast_to(v, (8, pheno)), 'sample', pairs)[:1]]
    ppermute x4, starting transfers between devices: 13.3 us -> 7.97 us  [step_fn(): lax.ppermute(msgs[k], 'sample', zone[d] if kind == 'in' else centre)]
    ppermute x3, starting transfers between devices: 3.24 us -> 8.07 us  [share_scale(): return lax.ppermute(jnp.broadcast_to(v, (8, pheno)), 'sample', pairs)[:1]]
    ppermute x8, waiting for transfers between devices: 18.7 us -> 21.9 us  [step_fn(): flight[k] = lax.ppermute(msgs[k], 'sample', pairs)]
    broadcast_in_dim x0 -> x1, other arithmetic: none -> 2.56 us  [step_fn(): return result[None]]
    convert_element_type x12 -> x13, other arithmetic: 9.11 us -> 7.78 us  [narrow(): return lax.reduce_precision(value, info.nexp, info.nmant).astype(dtype)]
    unnamed x11 -> x27, local copies, waits for them, and re-layouts: 5.35 us -> 4.96 us
  transfers between devices with their start and end apart: 38 -> 38, of which waited for: 15 -> 15; matrix products, arithmetic and copies ran while one was open for 22% -> 18% of each run, Pallas kernels for 1% -> 1%
where the time goes in v1:
time: 167 us
  waiting for transfers between devices  81 us (49%)
  starting transfers between devices  42 us (25%)
  other arithmetic  20.7 us (12%)
  matrix products  13.9 us (8%)
  local copies, waits for them, and re-layouts  6.95 us (4%)
    ppermute x23, waiting for transfers between devices, swap(): return lax.ppermute(value, axes, [(i, i ^ bit) for i in range(size)])  55.8 us
    ppermute x8, waiting for transfers between devices, step_fn(): flight[k] = lax.ppermute(msgs[k], 'sample', pairs)  21.9 us
    ppermute x23, starting transfers between devices, swap(): return lax.ppermute(value, axes, [(i, i ^ bit) for i in range(size)])  18.1 us
    dot_general x19, matrix products, dot_rows(): lax.dot_general(left, right, (((0,), (0,)), ((), ())), preferred_element_...  10.9 us
    ppermute x3, starting transfers between devices, share_scale(): return lax.ppermute(jnp.broadcast_to(v, (8, pheno)), 'sample', pairs)[:1]  8.07 us
    ppermute x4, starting transfers between devices, step_fn(): lax.ppermute(msgs[k], 'sample', zone[d] if kind == 'in' else centre)  7.97 us
    ppermute x8, starting transfers between devices, step_fn(): flight[k] = lax.ppermute(msgs[k], 'sample', pairs)  7.88 us
    convert_element_type x13, other arithmetic, narrow(): return lax.reduce_precision(value, info.nexp, info.nmant).astype(dtype)  7.78 us
  transfers between devices with their start and end apart: 38, of which 15 were waited for; matrix products, arithmetic and copies ran while one was open for 18% of the time, Pallas kernels for 1%

profile of v1, /device:TPU:0, one launch (start us, length us, event | category | flops | bytes accessed | tf_op | source)
XLA Modules:
  0.0 166.7 jit_solution(11687507658269176679)
XLA Ops:
  1.2 3.0 %collective-permute-start = (bf16[512,256]{1,0:T(8,128)(2,1)S(1)}, bf16[512,256]{1,0:T(8,128)(2,1)S(1)}, u32[]{:S(2)}, u32[]{:S(2)}) collective-permute-start(bf16[512,256]{1,0:T(8,128)(2,1)S(1)} %fusion.32), channel_id=1, source_target_pairs={{0,16},{16,0},{1,17},{17,1},{2,18},{18,2},{3,19},{19,3},{4,20},{20... | collective-permute-start | bytes 786440 | tf_op jit(solution)/shard_map/ppermute | solution.py:22
  4.2 3.0 %fusion.1 = bf16[256,4096]{1,0:T(8,128)(2,1)S(1)} fusion(bf16[1,256,4096]{2,1,0:T(8,128)(2,1)} %param.11, bf16[1,256,4096]{2,1,0:T(8,128)(2,1)} %param.12), kind=kLoop, calls=%fused_computation.2 | loop fusion | flops 5242880 | bytes 6291456 | tf_op jit(solution)/shard_map/convert_element_type | solution.py:31
  11.0 2.4 %subtract_bitcast_fusion.1 = f32[4096,256]{1,0:T(8,128)} fusion(f32[1,4096,256]{2,1,0:T(8,128)S(1)} %copy-done.4, bf16[1,4096,256]{2,1,0:T(8,128)(2,1)S(1)} %copy-done.9), kind=kLoop, calls=%fused_computation.4 | loop fusion | flops 3145728 | bytes 10485760 | tf_op jit(solution)/shard_map/sub | solution.py:129
  14.3 1.6 collective-permute-start.1
  15.9 2.6 %collective-permute-start.2 = (bf16[512,256]{1,0:T(8,128)(2,1)}, bf16[512,256]{1,0:T(8,128)(2,1)S(1)}, u32[]{:S(2)}, u32[]{:S(2)}) collective-permute-start(bf16[512,256]{1,0:T(8,128)(2,1)} %get-tuple-element.76), channel_id=1, source_target_pairs={{0,8},{2,10},{4,12},{6,14},{8,0},{10,2},{12,4},{14,6},{1,9},{3,11}... | collective-permute-start | bytes 786440 | tf_op jit(solution)/shard_map/ppermute | solution.py:22
  18.7 3.0 %broadcast_select_fusion.5 = (bf16[256,2048]{1,0:T(8,128)(2,1)}, bf16[256,2048]{1,0:T(8,128)(2,1)}) fusion(pred[]{:T(512)S(6)} %eq.13, bf16[256,4096]{1,0:T(8,128)(2,1)} %bitcast.111), kind=kLoop, calls=%fused_computation.19 | loop fusion | flops 1048576 | bytes 4194305 | tf_op jit(solution)/shard_map/jit(_where)/select_n | solution.py:100
  21.7 1.5 pack_rows.1
  23.2 3.8 %collective-permute-done.1 = bf16[512,256]{1,0:T(8,128)(2,1)S(1)} collective-permute-done((bf16[512,256]{1,0:T(8,128)(2,1)}, bf16[512,256]{1,0:T(8,128)(2,1)S(1)}, u32[]{:S(2)}, u32[]{:S(2)}) %collective-permute-start.1) | collective-permute-done | bytes 262176 | tf_op jit(solution)/shard_map/ppermute | solution.py:22
  27.1 10.4 %collective-permute-done.2 = bf16[512,256]{1,0:T(8,128)(2,1)S(1)} collective-permute-done((bf16[512,256]{1,0:T(8,128)(2,1)}, bf16[512,256]{1,0:T(8,128)(2,1)S(1)}, u32[]{:S(2)}, u32[]{:S(2)}) %collective-permute-start.2) | collective-permute-done | bytes 262176 | tf_op jit(solution)/shard_map/ppermute | solution.py:22
  41.8 2.2 %fusion.98 = f32[1024,256]{1,0:T(8,128)} fusion(bf16[256,1024]{1,0:T(8,128)(2,1)S(1)} %reduce-precision_convert_fusion.2, bf16[1,256,256]{2,1,0:T(8,128)(2,1)} %param.20), kind=kOutput, calls=%fused_computation.166 | convolution fusion | flops 134217728 | bytes 1703936 | tf_op jit(solution)/shard_map/dot_general | solution.py:43
  45.5 33.3 %collective-permute-done.6 = bf16[256,2048]{1,0:T(8,128)(2,1)S(1)} collective-permute-done((bf16[256,2048]{1,0:T(8,128)(2,1)S(1)}, bf16[256,2048]{1,0:T(8,128)(2,1)S(1)}, u32[]{:S(2)}, u32[]{:S(2)}) %collective-permute-start.6) | collective-permute-done | bytes 1048608 | tf_op jit(solution)/shard_map/ppermute | solution.py:22
  80.2 1.8 %fusion.104 = f32[2048,256]{1,0:T(8,128)} fusion(bf16[256,2048]{1,0:T(8,128)(2,1)S(1)} %reduce-precision_convert_fusion, bf16[256,256]{1,0:T(8,128)(2,1)S(1)} %collective-permute-done.10), kind=kOutput, calls=%fused_computation.172 | convolution fusion | flops 268435456 | bytes 3276800 | tf_op jit(solution)/shard_map/dot_general | solution.py:43
  88.3 1.9 %collective-permute-done.12 = f32[64,256]{1,0:T(8,128)S(1)} collective-permute-done((f32[64,256]{1,0:T(8,128)}, f32[64,256]{1,0:T(8,128)S(1)}, u32[]{:S(2)}, u32[]{:S(2)}) %collective-permute-start.12) | collective-permute-done | bytes 65568 | tf_op jit(solution)/shard_map/ppermute | solution.py:22
  91.2 1.8 %constant_dynamic-update-slice_fusion.7 = (bf16[256,256]{1,0:T(8,128)(2,1)S(1)}, bf16[64,256]{1,0:T(8,128)(2,1)}) fusion(bf16[256,256]{1,0:T(8,128)(2,1)S(1)} %broadcast_in_dim.29, s32[]{:T(128)S(6)} %select_n.126, bf16[384,256]{1,0:T(8,128)(2,1)} %collective-permute-done.14, f32[]{:T(128)S(6)} %sub.62, f32[]{:T(128)S(6)} %mul.347, ...), kind=kLoop, calls=%fused_computation.149 | loop fusion | flops 917504 | bytes 720916 | tf_op jit(solution)/shard_map/dynamic_update_slice | solution.py:170
  95.0 1.5 collective-permute-start.17
  98.5 1.5 collective-permute-done.17
  101.7 5.9 %collective-permute-start.19 = (f32[8,256]{1,0:T(8,128)S(1)}, f32[8,256]{1,0:T(8,128)S(1)}, u32[]{:S(2)}, u32[]{:S(2)}) collective-permute-start(f32[8,256]{1,0:T(8,128)S(1)} %broadcast_in_dim.31), channel_id=1, source_target_pairs={{0,4},{2,6},{12,8},{14,10},{1,5},{3,7},{13,9},{15,11},{16,20},{18,... | collective-permute-start | bytes 24584 | tf_op jit(solution)/shard_map/ppermute | solution.py:192
  118.0 4.0 %collective-permute-start.30 = (f16[512,256]{1,0:T(8,128)(2,1)S(1)}, f16[512,256]{1,0:T(8,128)(2,1)S(1)}, u32[]{:S(2)}, u32[]{:S(2)}) collective-permute-start(f16[512,256]{1,0:T(8,128)(2,1)S(1)} %get-tuple-element.100), channel_id=1, source_target_pairs={{0,4},{2,6},{12,8},{14,10},{1,5},{3,7},{13,9},{15,11},{16,20},{18,... | collective-permute-start | bytes 786440 | tf_op jit(solution)/shard_map/ppermute | solution.py:236
  124.4 3.2 %collective-permute-done.21 = f32[8,256]{1,0:T(8,128)S(1)} collective-permute-done((f32[8,256]{1,0:T(8,128)S(1)}, f32[8,256]{1,0:T(8,128)S(1)}, u32[]{:S(2)}, u32[]{:S(2)}) %collective-permute-start.21) | collective-permute-done | bytes 8224 | tf_op jit(solution)/shard_map/ppermute | solution.py:192
  133.0 11.1 %collective-permute-done.25 = f16[512,256]{1,0:T(8,128)(2,1)S(1)} collective-permute-done((f16[512,256]{1,0:T(8,128)(2,1)S(1)}, f16[512,256]{1,0:T(8,128)(2,1)S(1)}, u32[]{:S(2)}, u32[]{:S(2)}) %collective-permute-start.25) | collective-permute-done | bytes 262176 | tf_op jit(solution)/shard_map/ppermute | solution.py:254
  146.9 3.9 %collective-permute-done.28 = f16[512,256]{1,0:T(8,128)(2,1)S(1)} collective-permute-done((f16[512,256]{1,0:T(8,128)(2,1)S(1)}, f16[512,256]{1,0:T(8,128)(2,1)S(1)}, u32[]{:S(2)}, u32[]{:S(2)}) %collective-permute-start.28) | collective-permute-done | bytes 262176 | tf_op jit(solution)/shard_map/ppermute | solution.py:254
  153.2 2.1 %collective-permute-done.31 = f16[512,256]{1,0:T(8,128)(2,1)S(1)} collective-permute-done((f16[512,256]{1,0:T(8,128)(2,1)S(1)}, f16[512,256]{1,0:T(8,128)(2,1)S(1)}, u32[]{:S(2)}, u32[]{:S(2)}) %collective-permute-start.31) | collective-permute-done | bytes 262176 | tf_op jit(solution)/shard_map/ppermute | solution.py:254
  155.4 4.8 %collective-permute-done.33 = f16[512,256]{1,0:T(8,128)(2,1)S(1)} collective-permute-done((f16[512,256]{1,0:T(8,128)(2,1)S(1)}, f16[512,256]{1,0:T(8,128)(2,1)S(1)}, u32[]{:S(2)}, u32[]{:S(2)}) %collective-permute-start.33) | collective-permute-done | bytes 262176 | tf_op jit(solution)/shard_map/ppermute | solution.py:254
  164.2 2.6 %subtract_bitcast_fusion = f32[1,4096,256]{2,1,0:T(8,128)} fusion(f32[4096,256]{1,0:T(8,128)S(1)} %copy-done, f16[2048,256]{1,0:T(8,128)(2,1)S(1)} %get-tuple-element.78, f16[2048,256]{1,0:T(8,128)(2,1)S(1)} %get-tuple-element.77, f32[256]{0:T(256)S(1)} %bitcast.136), kind=kLoop, calls=%fused_computation.3 | loop fusion | flops 4194304 | bytes 10486784 | tf_op jit(solution)/shard_map/broadcast_in_dim | solution.py:262
  (151 shorter events, 52.8 us)
Async XLA Ops:
  1.2 12.3 %collective-permute-start = (bf16[512,256]{1,0:T(8,128)(2,1)S(1)}, bf16[512,256]{1,0:T(8,128)(2,1)S(1)}, u32[]{:S(2)}, u32[]{:S(2)}) collective-permute-start(bf16[512,256]{1,0:T(8,128)(2,1)S(1)} %fusion.32), channel_id=1, source_target_pairs={{0,16},{16,0},{1,17},{17,1},{2,18},{18,2},{3,19},{19,3},{4,20},{20... | collective-permute-start | bytes 786440 | tf_op jit(solution)/shard_map/ppermute | solution.py:22
  9.5 28.7 %collective-permute-start.4 = (bf16[256,1024]{1,0:T(8,128)(2,1)}, bf16[256,1024]{1,0:T(8,128)(2,1)S(1)}, u32[]{:S(2)}, u32[]{:S(2)}) collective-permute-start(bf16[256,1024]{1,0:T(8,128)(2,1)} %get-tuple-element.83), channel_id=1, source_target_pairs={{0,16},{16,0},{1,17},{17,1},{2,18},{18,2},{3,19},{19,3},{4,20},{20... | collective-permute-start | bytes 1572872 | tf_op jit(solution)/shard_map/ppermute | solution.py:22
  9.5 70.7 %collective-permute-start.10 = (bf16[256,256]{1,0:T(8,128)(2,1)}, bf16[256,256]{1,0:T(8,128)(2,1)S(1)}, u32[]{:S(2)}, u32[]{:S(2)}) collective-permute-start(bf16[256,256]{1,0:T(8,128)(2,1)} %bitcast.6.refs_5_), channel_id=1, source_target_pairs={{0,2},{2,0},{4,6},{6,4},{8,10},{10,8},{12,14},{14,12},{1,3},{3,1},... | collective-permute-start | bytes 393224 | tf_op jit(solution)/shard_map/ppermute | solution.py:22
  14.3 12.7 %collective-permute-start.1 = (bf16[512,256]{1,0:T(8,128)(2,1)}, bf16[512,256]{1,0:T(8,128)(2,1)S(1)}, u32[]{:S(2)}, u32[]{:S(2)}) collective-permute-start(bf16[512,256]{1,0:T(8,128)(2,1)} %get-tuple-element.76), channel_id=1, source_target_pairs={{0,4},{2,6},{4,0},{6,2},{8,12},{10,14},{12,8},{14,10},{1,5},{3,7},... | collective-permute-start | bytes 786440 | tf_op jit(solution)/shard_map/ppermute | solution.py:22
  15.9 21.5 %collective-permute-start.2 = (bf16[512,256]{1,0:T(8,128)(2,1)}, bf16[512,256]{1,0:T(8,128)(2,1)S(1)}, u32[]{:S(2)}, u32[]{:S(2)}) collective-permute-start(bf16[512,256]{1,0:T(8,128)(2,1)} %get-tuple-element.76), channel_id=1, source_target_pairs={{0,8},{2,10},{4,12},{6,14},{8,0},{10,2},{12,4},{14,6},{1,9},{3,11}... | collective-permute-start | bytes 786440 | tf_op jit(solution)/shard_map/ppermute | solution.py:22
  18.5 19.0 %collective-permute-start.3 = (bf16[512,256]{1,0:T(8,128)(2,1)}, bf16[512,256]{1,0:T(8,128)(2,1)S(1)}, u32[]{:S(2)}, u32[]{:S(2)}) collective-permute-start(bf16[512,256]{1,0:T(8,128)(2,1)} %get-tuple-element.76), channel_id=1, source_target_pairs={{0,12},{2,14},{4,8},{6,10},{8,4},{10,6},{12,0},{14,2},{1,13},{3,15... | collective-permute-start | bytes 786440 | tf_op jit(solution)/shard_map/ppermute | solution.py:22
  27.0 17.4 %collective-permute-start.7 = (bf16[256,2048]{1,0:T(8,128)(2,1)}, bf16[256,2048]{1,0:T(8,128)(2,1)S(1)}, u32[]{:S(2)}, u32[]{:S(2)}) collective-permute-start(bf16[256,2048]{1,0:T(8,128)(2,1)} %get-tuple-element.80), channel_id=1, source_target_pairs={{0,2},{2,0},{4,6},{6,4},{8,10},{10,8},{12,14},{14,12},{1,3},{3,1},... | collective-permute-start | bytes 3145736 | tf_op jit(solution)/shard_map/ppermute | solution.py:22
  37.5 44.6 %collective-permute-start.9 = (bf16[256,1024]{1,0:T(8,128)(2,1)}, bf16[256,1024]{1,0:T(8,128)(2,1)S(1)}, u32[]{:S(2)}, u32[]{:S(2)}) collective-permute-start(bf16[256,1024]{1,0:T(8,128)(2,1)} %get-tuple-element.84), channel_id=1, source_target_pairs={{0,16},{16,0},{1,17},{17,1},{2,18},{18,2},{3,19},{19,3},{4,20},{20... | collective-permute-start | bytes 1572872 | tf_op jit(solution)/shard_map/ppermute | solution.py:22
  38.1 49.0 %collective-permute-start.14 = (bf16[384,256]{1,0:T(8,128)(2,1)}, bf16[384,256]{1,0:T(8,128)(2,1)}, u32[]{:S(2)}, u32[]{:S(2)}) collective-permute-start(bf16[384,256]{1,0:T(8,128)(2,1)} %pack_rows.1), channel_id=1, source_target_pairs={{0,16},{16,0},{1,17},{17,1},{2,18},{18,2},{3,19},{19,3},{4,20},{20... | collective-permute-start | bytes 589832 | tf_op jit(solution)/shard_map/ppermute | solution.py:22
  40.3 38.5 %collective-permute-start.6 = (bf16[256,2048]{1,0:T(8,128)(2,1)S(1)}, bf16[256,2048]{1,0:T(8,128)(2,1)S(1)}, u32[]{:S(2)}, u32[]{:S(2)}) collective-permute-start(bf16[256,2048]{1,0:T(8,128)(2,1)S(1)} %collective-permute-done.5), channel_id=1, source_target_pairs={{0,16},{16,0},{1,17},{17,1},{2,18},{18,2},{3,19},{19,3},{4,20},{20... | collective-permute-start | bytes 3145736 | tf_op jit(solution)/shard_map/ppermute | solution.py:22
  101.7 14.9 %collective-permute-start.19 = (f32[8,256]{1,0:T(8,128)S(1)}, f32[8,256]{1,0:T(8,128)S(1)}, u32[]{:S(2)}, u32[]{:S(2)}) collective-permute-start(f32[8,256]{1,0:T(8,128)S(1)} %broadcast_in_dim.31), channel_id=1, source_target_pairs={{0,4},{2,6},{12,8},{14,10},{1,5},{3,7},{13,9},{15,11},{16,20},{18,... | collective-permute-start | bytes 24584 | tf_op jit(solution)/shard_map/ppermute | solution.py:192
  109.0 14.3 %collective-permute-start.22 = (f16[512,256]{1,0:T(8,128)(2,1)S(1)}, f16[512,256]{1,0:T(8,128)(2,1)S(1)}, u32[]{:S(2)}, u32[]{:S(2)}) collective-permute-start(f16[512,256]{1,0:T(8,128)(2,1)S(1)} %get-tuple-element.94), channel_id=1, source_target_pairs={{0,4},{2,6},{12,8},{14,10},{1,5},{3,7},{13,9},{15,11},{16,20},{18,... | collective-permute-start | bytes 786440 | tf_op jit(solution)/shard_map/ppermute | solution.py:236
  111.7 15.9 %collective-permute-start.24 = (f16[512,256]{1,0:T(8,128)(2,1)S(1)}, f16[512,256]{1,0:T(8,128)(2,1)S(1)}, u32[]{:S(2)}, u32[]{:S(2)}) collective-permute-start(f16[512,256]{1,0:T(8,128)(2,1)S(1)} %get-tuple-element.96), channel_id=1, source_target_pairs={{0,4},{2,6},{12,8},{14,10},{1,5},{3,7},{13,9},{15,11},{16,20},{18,... | collective-permute-start | bytes 786440 | tf_op jit(solution)/shard_map/ppermute | solution.py:236
  114.4 15.9 %collective-permute-start.27 = (f16[512,256]{1,0:T(8,128)(2,1)S(1)}, f16[512,256]{1,0:T(8,128)(2,1)S(1)}, u32[]{:S(2)}, u32[]{:S(2)}) collective-permute-start(f16[512,256]{1,0:T(8,128)(2,1)S(1)} %get-tuple-element.98), channel_id=1, source_target_pairs={{0,4},{2,6},{12,8},{14,10},{1,5},{3,7},{13,9},{15,11},{16,20},{18,... | collective-permute-start | bytes 786440 | tf_op jit(solution)/shard_map/ppermute | solution.py:236
  118.0 26.2 %collective-permute-start.30 = (f16[512,256]{1,0:T(8,128)(2,1)S(1)}, f16[512,256]{1,0:T(8,128)(2,1)S(1)}, u32[]{:S(2)}, u32[]{:S(2)}) collective-permute-start(f16[512,256]{1,0:T(8,128)(2,1)S(1)} %get-tuple-element.100), channel_id=1, source_target_pairs={{0,4},{2,6},{12,8},{14,10},{1,5},{3,7},{13,9},{15,11},{16,20},{18,... | collective-permute-start | bytes 786440 | tf_op jit(solution)/shard_map/ppermute | solution.py:236
  122.1 5.5 %collective-permute-start.21 = (f32[8,256]{1,0:T(8,128)S(1)}, f32[8,256]{1,0:T(8,128)S(1)}, u32[]{:S(2)}, u32[]{:S(2)}) collective-permute-start(f32[8,256]{1,0:T(8,128)S(1)} %broadcast_in_dim.35), channel_id=1, source_target_pairs={{4,0},{6,2},{8,12},{10,14},{5,1},{7,3},{9,13},{11,15},{20,16},{22,... | collective-permute-start | bytes 24584 | tf_op jit(solution)/shard_map/ppermute | solution.py:192
  129.0 15.1 %collective-permute-start.25 = (f16[512,256]{1,0:T(8,128)(2,1)S(1)}, f16[512,256]{1,0:T(8,128)(2,1)S(1)}, u32[]{:S(2)}, u32[]{:S(2)}) collective-permute-start(f16[512,256]{1,0:T(8,128)(2,1)S(1)} %reduce-precision_convert_fusion.8), channel_id=1, source_target_pairs={{4,0},{6,2},{8,12},{10,14},{5,1},{7,3},{9,13},{11,15},{20,16},{22,... | collective-permute-start | bytes 786440 | tf_op jit(solution)/shard_map/ppermute | solution.py:254
  130.7 14.6 %collective-permute-start.29 = (f16[512,256]{1,0:T(8,128)(2,1)S(1)}, f16[512,256]{1,0:T(8,128)(2,1)S(1)}, u32[]{:S(2)}, u32[]{:S(2)}) collective-permute-start(f16[512,256]{1,0:T(8,128)(2,1)S(1)} %reduce-precision_convert_fusion.7), channel_id=1, source_target_pairs={{4,8},{6,10},{8,4},{10,6},{5,9},{7,11},{9,5},{11,7},{20,24},{22,26... | collective-permute-start | bytes 786440 | tf_op jit(solution)/shard_map/ppermute | solution.py:254
  131.7 19.1 %collective-permute-start.28 = (f16[512,256]{1,0:T(8,128)(2,1)S(1)}, f16[512,256]{1,0:T(8,128)(2,1)S(1)}, u32[]{:S(2)}, u32[]{:S(2)}) collective-permute-start(f16[512,256]{1,0:T(8,128)(2,1)S(1)} %reduce-precision_convert_fusion.6), channel_id=1, source_target_pairs={{4,0},{6,2},{8,12},{10,14},{5,1},{7,3},{9,13},{11,15},{20,16},{22,... | collective-permute-start | bytes 786440 | tf_op jit(solution)/shard_map/ppermute | solution.py:254
  144.5 6.4 %collective-permute-start.32 = (f16[512,256]{1,0:T(8,128)(2,1)S(1)}, f16[512,256]{1,0:T(8,128)(2,1)S(1)}, u32[]{:S(2)}, u32[]{:S(2)}) collective-permute-start(f16[512,256]{1,0:T(8,128)(2,1)S(1)} %reduce-precision_convert_fusion.5), channel_id=1, source_target_pairs={{4,8},{6,10},{8,4},{10,6},{5,9},{7,11},{9,5},{11,7},{20,24},{22,26... | collective-permute-start | bytes 786440 | tf_op jit(solution)/shard_map/ppermute | solution.py:254
  145.6 9.7 %collective-permute-start.31 = (f16[512,256]{1,0:T(8,128)(2,1)S(1)}, f16[512,256]{1,0:T(8,128)(2,1)S(1)}, u32[]{:S(2)}, u32[]{:S(2)}) collective-permute-start(f16[512,256]{1,0:T(8,128)(2,1)S(1)} %reduce-precision_convert_fusion.4), channel_id=1, source_target_pairs={{4,0},{6,2},{8,12},{10,14},{5,1},{7,3},{9,13},{11,15},{20,16},{22,... | collective-permute-start | bytes 786440 | tf_op jit(solution)/shard_map/ppermute | solution.py:254
  151.3 9.0 %collective-permute-start.33 = (f16[512,256]{1,0:T(8,128)(2,1)S(1)}, f16[512,256]{1,0:T(8,128)(2,1)S(1)}, u32[]{:S(2)}, u32[]{:S(2)}) collective-permute-start(f16[512,256]{1,0:T(8,128)(2,1)S(1)} %reduce-precision_convert_fusion.3), channel_id=1, source_target_pairs={{4,0},{6,2},{8,12},{10,14},{5,1},{7,3},{9,13},{11,15},{20,16},{22,... | collective-permute-start | bytes 786440 | tf_op jit(solution)/shard_map/ppermute | solution.py:254
  152.6 7.9 %collective-permute-start.35 = (f16[512,256]{1,0:T(8,128)(2,1)S(1)}, f16[512,256]{1,0:T(8,128)(2,1)S(1)}, u32[]{:S(2)}, u32[]{:S(2)}) collective-permute-start(f16[512,256]{1,0:T(8,128)(2,1)S(1)} %broadcast_select_fusion.8), channel_id=1, source_target_pairs={{0,2},{2,0},{4,6},{6,4},{8,10},{10,8},{12,14},{14,12},{1,3},{3,1},... | collective-permute-start | bytes 786440 | tf_op jit(solution)/shard_map/ppermute | solution.py:22
  152.7 7.8 %collective-permute-start.34 = (f16[512,256]{1,0:T(8,128)(2,1)S(1)}, f16[512,256]{1,0:T(8,128)(2,1)S(1)}, u32[]{:S(2)}, u32[]{:S(2)}) collective-permute-start(f16[512,256]{1,0:T(8,128)(2,1)S(1)} %broadcast_select_fusion.9), channel_id=1, source_target_pairs={{0,2},{2,0},{4,6},{6,4},{8,10},{10,8},{12,14},{14,12},{1,3},{3,1},... | collective-permute-start | bytes 786440 | tf_op jit(solution)/shard_map/ppermute | solution.py:22
  (26 other events, 121.5 us)
